TPU v7x, 32 devices: a whole 2x2x4 slice. The times are simulated.
32 devices in a mesh: tm: 8 (over y, x, core), floor: 4 (over z).
Axes of the slice: x: 2, y: 2, z: 4, core: 2. Of those that a mesh axis runs over, the one named last changes fastest.
Arguments:
- samples: bfloat16 [8, 16, 32768], P('tm', None, 'floor'), may hold values from -6 to 6
- operator: bfloat16 [8, 512, 32768], P('tm', None, 'floor'), may hold values from -0.01171875 to 0.01171875
Outputs:
- sensor_data: bfloat16 [8, 16, 512], P('tm', None, 'floor')
All inputs are finite; a program needn't handle non-finite values.
Results may differ from a plain program's by a relative error of at most 0.0013.
Values may be sent and summed in bfloat16 or wider, within the bound.
A program may use at most 64 MiB of HBM per device.

v0:
```python
import jax
import jax.numpy as jnp
from jax import lax
from jax.sharding import PartitionSpec as P


def local(samples, operator):
    lag = lax.axis_index("tm")
    blocks = lax.axis_size("tm")
    kernel = operator[0]
    images = jnp.einsum(
        "cki,si->cks",
        lax.all_gather(samples, "tm", axis=0, tiled=True),
        kernel,
        preferred_element_type=jnp.float32,
    )
    padded = jnp.pad(images, ((blocks, 0), (0, 0), (0, 0)))
    shifted = lax.dynamic_slice_in_dim(padded, blocks - lag, blocks, 0)
    shares = lax.psum_scatter(shifted, "floor", scatter_dimension=2, tiled=True)
    records = lax.psum_scatter(shares, "tm", scatter_dimension=0, tiled=True)
    return records.astype(jnp.bfloat16)


def solution(mesh):
    placed = (P("tm", None, "floor"), P("tm", None, "floor"))
    return jax.shard_map(
        local, mesh=mesh, in_specs=placed, out_specs=P("tm", None, "floor"), check_vma=False
    )
```

profile of v0, /device:TPU:0, one launch (start us, length us, event | category | flops | bytes accessed | tf_op | source)
XLA Modules:
  0.0 109.7 jit_solution(5903689405947490531)
XLA Ops:
  6.5 0.0 all-gather.2.cloned.1.call-start
  6.5 0.7 all-gather.2.cloned.1.call-update
  7.3 0.0 reduce-scatter.3.cloned.1.call-start
  7.3 32.4 %all-gather.2.cloned.1.call-done = bf16[8,16,8192]{2,1,0:T(8,128)(2,1)} async-done(((bf16[1,16,8192]{2,1,0:T(8,128)(2,1)}), bf16[8,16,8192]{2,1,0:T(8,128)(2,1)}) %all-gather.2.cloned.1.call-update) | async-done | bytes 2097168 | tf_op jit(solution)/shard_map/all_gather | solution.py:13
  39.8 6.4 %fusion = f32[16,16,512]{2,1,0:T(8,128)S(1)} fusion(bf16[8,16,8192]{2,1,0:T(8,128)(2,1)} %all-gather.2.cloned.1.call-done, bf16[1,512,8192]{2,1,0:T(8,128)(2,1)} %param.3), kind=kOutput, calls=%fused_computation | convolution fusion | flops 1073741824 | bytes 11010048 | tf_op jit(solution)/shard_map/jit(_pad)/pad | solution.py:17
  46.1 0.7 constant_dynamic-slice_fusion
  46.9 0.0 reduce-scatter.3.cloned.1.call-update
  46.9 0.0 reduce-scatter.5.cloned.1.call-start
  46.9 20.1 %reduce-scatter.3.cloned.1.call-done = f32[8,16,128]{2,1,0:T(8,128)} async-done(((f32[8,16,512]{2,1,0:T(8,128)}), f32[8,16,128]{2,1,0:T(8,128)}) %reduce-scatter.3.cloned.1.call-update) | async-done | bytes 65552 | tf_op jit(solution)/shard_map/reduce_scatter | solution.py:19
  67.0 0.0 reduce-scatter.5.cloned.1.call-update
  67.0 34.8 %reduce-scatter.5.cloned.1.call-done = f32[1,16,128]{2,1,0:T(8,128)} async-done(((f32[8,16,128]{2,1,0:T(8,128)}), f32[1,16,128]{2,1,0:T(8,128)}) %reduce-scatter.5.cloned.1.call-update) | async-done | bytes 8208 | tf_op jit(solution)/shard_map/reduce_scatter | solution.py:20
  101.8 1.3 %convert_element_type.5 = bf16[1,16,128]{2,1,0:T(8,128)(2,1)} convert(f32[1,16,128]{2,1,0:T(8,128)} %reduce-scatter.5.cloned.1.call-done) | non-fusion elementwise | flops 2048 | bytes 12288 | tf_op jit(solution)/shard_map/convert_element_type | solution.py:21
Async XLA Ops:
  6.5 33.2 %all-gather.2.cloned.1.call-start = ((), (), s32[]{:S(2)}) async-start(), calls=%async_computation.2 | async-start | bytes 2359296 | tf_op jit(solution)/shard_map/all_gather | solution.py:13
  7.3 59.8 %reduce-scatter.3.cloned.1.call-start = ((), (), s32[]{:S(2)}) async-start(), calls=%async_computation.3 | async-start | bytes 327680 | tf_op jit(solution)/shard_map/reduce_scatter | solution.py:19
  46.9 55.0 %reduce-scatter.5.cloned.1.call-start = ((), (), s32[]{:S(2)}) async-start(), calls=%async_computation.4 | async-start | bytes 73728 | tf_op jit(solution)/shard_map/reduce_scatter | solution.py:20
Sparse Core Ops, SparseCore 0:
  9.2 30.4 all-gather.1
  47.0 19.9 reduce-scatter.2
  70.0 31.7 reduce-scatter.4
where the time goes:
time: 110 us
  waiting for transfers between devices  88.1 us (80%)
  between operations  13.1 us (12%)
  matrix products  6.37 us (6%)
  other arithmetic  1.29 us (1%)
    reduce_scatter x1, waiting for transfers between devices, local(): records = lax.psum_scatter(shares, 'tm', scatter_dimension=0, tiled=True)  34.8 us
    all_gather x1, waiting for transfers between devices, local(): lax.all_gather(samples, 'tm', axis=0, tiled=True)  32.4 us
    reduce_scatter x1, waiting for transfers between devices, local(): shares = lax.psum_scatter(shifted, 'floor', scatter_dimension=2, tiled=True)  20.1 us
    pad x1, matrix products, local(): padded = jnp.pad(images, ((blocks, 0), (0, 0), (0, 0)))  6.37 us
  transfers between devices with their start and end apart: 3, of which 3 were waited for; matrix products, arithmetic and copies ran while one was open for 0% of the time, Pallas kernels for 0%

commit v1 on v0

v1 whole, which is shorter than its diff:
```python
import functools

import jax
import jax.numpy as jnp
from jax import lax
from jax.experimental import pallas as pl
from jax.experimental.pallas import tpu as pltpu
from jax.sharding import PartitionSpec as P

MESH = pl.DeviceIdType.MESH


def kernel(
    n, m, chunks, x_hbm, op_hbm, out_ref, x, op, acc, part, total, share,
    own_sem, op_sem, out_sem, pair_sem, fwd_sem, in_sem,
    red_out, red_in, floor_out, floor_in,
):
    me, floor = lax.axis_index("tm"), lax.axis_index("floor")
    chips = n // 2
    chip, core = lax.div(me, 2), lax.rem(me, 2)
    pair = 2 * chip + 1 - core
    k, width = x.shape[2], x.shape[3]
    sensors = op.shape[1]
    share_size = sensors // m

    def columns(c):
        return pl.ds(c * width, width)

    own = [pltpu.make_async_copy(x_hbm.at[0, :, columns(c)], x.at[c, me], own_sem.at[c]) for c in range(chunks)]
    weights = [pltpu.make_async_copy(op_hbm.at[0, :, columns(c)], op.at[c], op_sem.at[c]) for c in range(chunks)]
    for c in range(chunks):
        own[c].start()
        weights[c].start()

    barrier = pltpu.get_barrier_semaphore()
    for step in range(1, n):
        pl.semaphore_signal(barrier, inc=1, device_id={"tm": lax.rem(me + step, n)}, device_id_type=MESH)
    for step in range(1, m):
        pl.semaphore_signal(barrier, inc=1, device_id={"floor": lax.rem(floor + step, m)}, device_id_type=MESH)
    pl.semaphore_wait(barrier, n + m - 2)

    def need(block, at_chip):
        return 2 * at_chip + block < n

    def to_chip(c, step):
        other = lax.rem(chip + step, chips)
        copy = pltpu.make_async_remote_copy(
            src_ref=x_hbm.at[0, :, columns(c)], dst_ref=x.at[c, me],
            send_sem=out_sem.at[c, step], recv_sem=in_sem.at[c, me],
            device_id={"tm": 2 * other + core}, device_id_type=MESH,
        )
        return need(me, other), copy

    def to_pair(c):
        copy = pltpu.make_async_remote_copy(
            src_ref=x_hbm.at[0, :, columns(c)], dst_ref=x.at[c, me],
            send_sem=pair_sem.at[c], recv_sem=in_sem.at[c, me],
            device_id={"tm": pair}, device_id_type=MESH,
        )
        return need(me, chip), copy

    def forward(c, block):
        return pltpu.make_async_remote_copy(
            src_ref=x.at[c, block], dst_ref=x.at[c, block],
            send_sem=fwd_sem.at[c, block], recv_sem=in_sem.at[c, block],
            device_id={"tm": pair}, device_id_type=MESH,
        )

    def sends(act):
        for c in range(chunks):
            for step in range(chips - 1, 0, -1):
                wanted, copy = to_chip(c, step)
                pl.when(wanted)(functools.partial(act, copy))
            wanted, copy = to_pair(c)
            pl.when(wanted)(functools.partial(act, copy))

    sends(lambda copy: copy.start())

    def take_and_forward(c):
        for step in range(1, chips):
            block = 2 * lax.rem(chip + step, chips) + core

            @pl.when(need(block, chip))
            def _():
                copy = forward(c, block)
                copy.wait_recv()
                copy.start()

    def take(c):
        for step in range(chips):
            block = 2 * lax.rem(chip + step, chips) + 1 - core

            @pl.when(need(block, chip))
            def _():
                forward(c, block).wait_recv()

    tile = min(n, max(1, 128 // k))

    take_and_forward(0)
    for c in range(chunks):
        if c + 1 < chunks:
            take_and_forward(c + 1)
        take(c)
        own[c].wait()
        weights[c].wait()
        for r in range(n // tile):
            rows = x[c, r * tile:(r + 1) * tile].reshape(tile * k, width)
            image = lax.dot_general(
                rows, op[c], (((1,), (1,)), ((), ())), preferred_element_type=jnp.float32
            ).reshape(tile, k, sensors)
            if c == 0:
                acc[r * tile:(r + 1) * tile] = image
            else:
                acc[r * tile:(r + 1) * tile] += image

    def lag_part(step):
        return pltpu.make_async_remote_copy(
            src_ref=acc.at[step], dst_ref=part.at[me],
            send_sem=red_out.at[step], recv_sem=red_in.at[me],
            device_id={"tm": lax.rem(me + step, n)}, device_id_type=MESH,
        )

    for step in range(n - 1, 0, -1):
        @pl.when(me + step < n)
        def _(step=step):
            lag_part(step).start()

    def add_lag(lag, value):
        pltpu.make_async_remote_copy(
            src_ref=acc.at[0], dst_ref=part.at[lag],
            send_sem=red_out.at[0], recv_sem=red_in.at[lag],
            device_id={"tm": pair}, device_id_type=MESH,
        ).wait_recv()
        return value + part[lag]

    value = lax.fori_loop(0, me, add_lag, acc[0])
    for j in range(m):
        total[j] = value[:, j * share_size:(j + 1) * share_size]

    def to_floor(step):
        other = lax.rem(floor + step, m)
        return pltpu.make_async_remote_copy(
            src_ref=total.at[other], dst_ref=share.at[floor],
            send_sem=floor_out.at[step], recv_sem=floor_in.at[floor],
            device_id={"floor": other}, device_id_type=MESH,
        )

    for step in range(m - 1, 0, -1):
        to_floor(step).start()
    result = total[floor]
    for step in range(1, m):
        source = lax.rem(floor + step, m)
        pltpu.make_async_remote_copy(
            src_ref=total.at[source], dst_ref=share.at[source],
            send_sem=floor_out.at[step], recv_sem=floor_in.at[source],
            device_id={"floor": source}, device_id_type=MESH,
        ).wait_recv()
        result = result + share[source]
    out_ref[0] = result.astype(out_ref.dtype)

    sends(lambda copy: copy.wait_send())
    for c in range(chunks):
        for step in range(1, chips):
            block = 2 * lax.rem(chip + step, chips) + core

            @pl.when(need(block, chip))
            def _(c=c, block=block):
                forward(c, block).wait_send()
    for step in range(n - 1, 0, -1):
        @pl.when(me + step < n)
        def _(step=step):
            lag_part(step).wait_send()
    for step in range(1, m):
        to_floor(step).wait_send()


def solution(mesh):
    n, m = mesh.shape["tm"], mesh.shape["floor"]

    def local(samples, operator):
        _, k, depth = samples.shape
        sensors = operator.shape[1]
        chunks = 8
        width = depth // chunks
        return pl.pallas_call(
            functools.partial(kernel, n, m, chunks),
            out_shape=jax.ShapeDtypeStruct((1, k, sensors // m), jnp.bfloat16),
            in_specs=[pl.BlockSpec(memory_space=pl.ANY)] * 2,
            out_specs=pl.BlockSpec(memory_space=pltpu.VMEM),
            scratch_shapes=[
                pltpu.VMEM((chunks, n, k, width), jnp.bfloat16),
                pltpu.VMEM((chunks, sensors, width), jnp.bfloat16),
                pltpu.VMEM((n, k, sensors), jnp.float32),
                pltpu.VMEM((n, k, sensors), jnp.float32),
                pltpu.VMEM((m, k, sensors // m), jnp.float32),
                pltpu.VMEM((m, k, sensors // m), jnp.float32),
                pltpu.SemaphoreType.DMA((chunks,)),
                pltpu.SemaphoreType.DMA((chunks,)),
                pltpu.SemaphoreType.DMA((chunks, n // 2)),
                pltpu.SemaphoreType.DMA((chunks,)),
                pltpu.SemaphoreType.DMA((chunks, n)),
                pltpu.SemaphoreType.DMA((chunks, n)),
                pltpu.SemaphoreType.DMA((n,)),
                pltpu.SemaphoreType.DMA((n,)),
                pltpu.SemaphoreType.DMA((m,)),
                pltpu.SemaphoreType.DMA((m,)),
            ],
            compiler_params=pltpu.CompilerParams(collective_id=0, has_side_effects=True),
        )(samples, operator)

    placed = (P("tm", None, "floor"), P("tm", None, "floor"))
    return jax.shard_map(
        local, mesh=mesh, in_specs=placed, out_specs=P("tm", None, "floor"), check_vma=False
    )
```

time: 110 us -> 30.9 us (0.28)
  the two profiles are of different devices: /device:TPU:0 before, /device:TPU:6 now
where the time goes in v1:
time: 30.9 us; the launch traced here: 30.4 us
  Pallas kernels  29.1 us (94%)
  local copies, waits for them, and re-layouts  1.28 us (4%)
    pallas_call x1, Pallas kernels, local(): pl.pallas_call(functools.partial(kernel, n, m, chunks), out_shape=jax.Sha...  29.1 us
    unnamed x1, local copies, waits for them, and re-layouts  1.28 us

profile of v1, /device:TPU:6, one launch (start us, length us, event | category | flops | bytes accessed | tf_op | source)
XLA Modules:
  0.0 30.4 jit_solution(2936932720743425163)
XLA Ops:
  0.0 29.1 %shard_map.28 = bf16[1,16,128]{2,1,0:T(8,128)(2,1)} custom-call(bf16[1,16,8192]{2,1,0:T(8,128)(2,1)} %x_hbm.1, bf16[1,512,8192]{2,1,0:T(8,128)(2,1)} %op_hbm.1), custom_call_target="tpu_custom_call" | custom-call | tf_op jit(solution)/shard_map/pallas_call | solution.py:185
  29.1 1.3 %copy.4 = bf16[1,16,128]{2,1,0:T(8,128)(2,1)} copy(bf16[1,16,128]{2,1,0:T(8,128)(2,1)} %shard_map.28) | data formatting | bytes 8192

commit v2 on v1

--- a/solution.py
+++ b/solution.py
@@ -8,16 +8,38 @@
 from jax.sharding import PartitionSpec as P
 
 MESH = pl.DeviceIdType.MESH
+AHEAD, LOOK = 4, 4
+
+
+def each(low, high, body):
+    if high - low <= 4:
+        for i in range(low, high):
+            body(i)
+    else:
+        def step(i, carry):
+            body(i)
+            return carry
+
+        lax.fori_loop(low, high, step, 0)
+
+
+def grid_of(chips):
+    rows = 1
+    while rows * rows * 4 <= chips and chips % (rows * 2) == 0:
+        rows *= 2
+    return rows, chips // rows
 
 
 def kernel(
     n, m, chunks, x_hbm, op_hbm, out_ref, x, op, acc, part, total, share,
-    own_sem, op_sem, out_sem, pair_sem, fwd_sem, in_sem,
+    own_sem, op_sem, out_sem, pair_sem, fwd_sem, relay_sem, in_sem,
     red_out, red_in, floor_out, floor_in,
 ):
     me, floor = lax.axis_index("tm"), lax.axis_index("floor")
     chips = n // 2
+    rows, cols = grid_of(chips)
     chip, core = lax.div(me, 2), lax.rem(me, 2)
+    row, col = lax.div(chip, cols), lax.rem(chip, cols)
     pair = 2 * chip + 1 - core
     k, width = x.shape[2], x.shape[3]
     sensors = op.shape[1]
@@ -42,71 +64,137 @@
     def need(block, at_chip):
         return 2 * at_chip + block < n
 
-    def to_chip(c, step):
+    many = max(rows, cols)
+
+    def relayed(odd, source, block, at, step):
+        turn = lax.rem(core + odd, 2) == 0
+        r, q = lax.div(source, cols), lax.rem(source, cols)
+        r_at, q_at = lax.div(at, cols), lax.rem(at, cols)
+        r_to, q_to = lax.rem(r + step, rows), lax.rem(q + step, cols)
+        down = (r_at == r) & (step < rows) & (turn | ((r_to == 0) & (q == 0)))
+        along = (q_at == q) & (step < cols) & (jnp.logical_not(turn) | ((q_to == 0) & (r == 0)))
+        target = jnp.where(r_at == r, r_to * cols + q_at, r_at * cols + q_to)
+        return (at != 0) & (down | along) & need(block, target), 2 * target + core
+
+    def route(odd, source, block, at):
+        passes = at < 0
+        for step in range(1, many):
+            passes = passes | relayed(odd, source, block, at, step)[0]
+        straight = (lax.div(source, cols) == lax.div(at, cols)) | (lax.rem(source, cols) == lax.rem(at, cols))
+        return straight & (need(block, at) | passes), passes
+
+    def make_plan(step, odd):
         other = lax.rem(chip + step, chips)
-        copy = pltpu.make_async_remote_copy(
-            src_ref=x_hbm.at[0, :, columns(c)], dst_ref=x.at[c, me],
-            send_sem=out_sem.at[c, step], recv_sem=in_sem.at[c, me],
-            device_id={"tm": 2 * other + core}, device_id_type=MESH,
+        block = 2 * other + core
+        wanted, _ = route(odd, chip, me, other)
+        _, passes = route(odd, other, block, chip)
+        here = need(block, chip)
+        alone = here & jnp.logical_not(passes)
+        onward = [relayed(odd, other, block, chip, s) for s in range(1, many)]
+        return other, block, wanted, passes, here, alone, onward
+
+    plans = {}
+    if chips <= 5:
+        plans = {(step, odd): make_plan(step, odd) for step in range(1, chips) for odd in (0, 1)}
+
+    def plan(step, c):
+        return plans[step, c % 2] if plans else make_plan(step, c % 2)
+
+    others = [2 * lax.rem(chip + step, chips) + 1 - core for step in range(chips)] if plans else None
+    others_here = [need(block, chip) for block in others] if plans else None
+    self_here = need(me, chip)
+
+    def send(c, block, target, sem, first=False):
+        return pltpu.make_async_remote_copy(
+            src_ref=x_hbm.at[0, :, columns(c)] if first else x.at[c, block], dst_ref=x.at[c, block],
+            send_sem=sem, recv_sem=in_sem.at[c, block], device_id={"tm": target}, device_id_type=MESH,
         )
-        return need(me, other), copy
-
-    def to_pair(c):
-        copy = pltpu.make_async_remote_copy(
-            src_ref=x_hbm.at[0, :, columns(c)], dst_ref=x.at[c, me],
-            send_sem=pair_sem.at[c], recv_sem=in_sem.at[c, me],
-            device_id={"tm": pair}, device_id_type=MESH,
-        )
-        return need(me, chip), copy
-
-    def forward(c, block):
-        return pltpu.make_async_remote_copy(
-            src_ref=x.at[c, block], dst_ref=x.at[c, block],
-            send_sem=fwd_sem.at[c, block], recv_sem=in_sem.at[c, block],
-            device_id={"tm": pair}, device_id_type=MESH,
-        )
-
-    def sends(act):
-        for c in range(chunks):
-            for step in range(chips - 1, 0, -1):
-                wanted, copy = to_chip(c, step)
-                pl.when(wanted)(functools.partial(act, copy))
-            wanted, copy = to_pair(c)
-            pl.when(wanted)(functools.partial(act, copy))
-
-    sends(lambda copy: copy.start())
-
-    def take_and_forward(c):
-        for step in range(1, chips):
-            block = 2 * lax.rem(chip + step, chips) + core
-
-            @pl.when(need(block, chip))
+
+    def sends(c, act):
+        def one(step):
+            _, block, wanted, *_ = plan(step, c)
+
+            @pl.when(wanted)
             def _():
-                copy = forward(c, block)
-                copy.wait_recv()
-                copy.start()
+                act(send(c, me, block, out_sem.at[c, step], True))
+
+        each(1, chips, one)
+
+        @pl.when(self_here)
+        def _():
+            act(send(c, me, pair, pair_sem.at[c], True))
+
+    def relays(c, act, wait):
+        def one(step):
+            source, block, _, passes, _, _, onward = plan(step, c)
+
+            @pl.when(passes)
+            def _():
+                if wait:
+                    send(c, block, pair, fwd_sem.at[c, source]).wait_recv()
+                for s, (wanted, target) in enumerate(onward):
+                    @pl.when(wanted)
+                    def _(s=s, target=target):
+                        act(send(c, block, target, relay_sem.at[c, source, s]))
+
+        each(1, chips, one)
+
+    def forwards(c, act, wait):
+        def one(step):
+            source, block, _, _, here, alone, _ = plan(step, c)
+            if wait:
+                @pl.when(alone)
+                def _():
+                    send(c, block, pair, fwd_sem.at[c, source]).wait_recv()
+
+            @pl.when(here)
+            def _():
+                act(send(c, block, pair, fwd_sem.at[c, source]))
+
+        each(1, chips, one)
 
     def take(c):
-        for step in range(chips):
-            block = 2 * lax.rem(chip + step, chips) + 1 - core
-
-            @pl.when(need(block, chip))
+        def one(step):
+            block = others[step] if plans else 2 * lax.rem(chip + step, chips) + 1 - core
+            here = others_here[step] if plans else need(block, chip)
+
+            @pl.when(here)
             def _():
-                forward(c, block).wait_recv()
+                send(c, block, pair, pair_sem.at[c]).wait_recv()
+
+        each(0, chips, one)
+
+    def start(copy):
+        copy.start()
+
+    def wait_send(copy):
+        copy.wait_send()
+
+    for c in range(min(AHEAD, chunks)):
+        sends(c, start)
 
     tile = min(n, max(1, 128 // k))
 
-    take_and_forward(0)
+    def pass_on(c):
+        if c < chunks:
+            relays(c, start, True)
+        if c + AHEAD < chunks:
+            sends(c + AHEAD, start)
+
+    for c in range(min(LOOK, chunks)):
+        pass_on(c)
+    forwards(0, start, True)
     for c in range(chunks):
+        pass_on(c + LOOK)
         if c + 1 < chunks:
-            take_and_forward(c + 1)
+            forwards(c + 1, start, True)
         take(c)
         own[c].wait()
         weights[c].wait()
         for r in range(n // tile):
-            rows = x[c, r * tile:(r + 1) * tile].reshape(tile * k, width)
+            block_rows = x[c, r * tile:(r + 1) * tile].reshape(tile * k, width)
             image = lax.dot_general(
-                rows, op[c], (((1,), (1,)), ((), ())), preferred_element_type=jnp.float32
+                block_rows, op[c], (((1,), (1,)), ((), ())), preferred_element_type=jnp.float32
             ).reshape(tile, k, sensors)
             if c == 0:
                 acc[r * tile:(r + 1) * tile] = image
@@ -124,6 +212,11 @@
         @pl.when(me + step < n)
         def _(step=step):
             lag_part(step).start()
+
+    for c in range(chunks):
+        sends(c, wait_send)
+        relays(c, wait_send, False)
+        forwards(c, wait_send, False)
 
     def add_lag(lag, value):
         pltpu.make_async_remote_copy(
@@ -158,14 +251,6 @@
         result = result + share[source]
     out_ref[0] = result.astype(out_ref.dtype)
 
-    sends(lambda copy: copy.wait_send())
-    for c in range(chunks):
-        for step in range(1, chips):
-            block = 2 * lax.rem(chip + step, chips) + core
-
-            @pl.when(need(block, chip))
-            def _(c=c, block=block):
-                forward(c, block).wait_send()
     for step in range(n - 1, 0, -1):
         @pl.when(me + step < n)
         def _(step=step):
@@ -180,7 +265,7 @@
     def local(samples, operator):
         _, k, depth = samples.shape
         sensors = operator.shape[1]
-        chunks = 8
+        chunks = 4
         width = depth // chunks
         return pl.pallas_call(
             functools.partial(kernel, n, m, chunks),
@@ -198,7 +283,8 @@
                 pltpu.SemaphoreType.DMA((chunks,)),
                 pltpu.SemaphoreType.DMA((chunks, n // 2)),
                 pltpu.SemaphoreType.DMA((chunks,)),
-                pltpu.SemaphoreType.DMA((chunks, n)),
+                pltpu.SemaphoreType.DMA((chunks, n // 2)),
+                pltpu.SemaphoreType.DMA((chunks, n // 2, max(1, max(grid_of(n // 2)) - 1))),
                 pltpu.SemaphoreType.DMA((chunks, n)),
                 pltpu.SemaphoreType.DMA((n,)),
                 pltpu.SemaphoreType.DMA((n,)),

time: 30.9 us -> 28.9 us (0.935)
  the two profiles are of different devices: /device:TPU:6 before, /device:TPU:2 now
where the time goes in v2:
time: 28.9 us; the launch traced here: 28.7 us
  Pallas kernels  27.4 us (95%)
  local copies, waits for them, and re-layouts  1.28 us (4%)
    pallas_call x1, Pallas kernels, local(): pl.pallas_call(functools.partial(kernel, n, m, chunks), out_shape=jax.Sha...  27.4 us
    unnamed x1, local copies, waits for them, and re-layouts  1.28 us

profile of v2, /device:TPU:2, one launch (start us, length us, event | category | flops | bytes accessed | tf_op | source)
XLA Modules:
  0.0 28.7 jit_solution(1397455405416147145)
XLA Ops:
  0.0 27.4 %shard_map.28 = bf16[1,16,128]{2,1,0:T(8,128)(2,1)} custom-call(bf16[1,16,8192]{2,1,0:T(8,128)(2,1)} %x_hbm.1, bf16[1,512,8192]{2,1,0:T(8,128)(2,1)} %op_hbm.1), custom_call_target="tpu_custom_call" | custom-call | tf_op jit(solution)/shard_map/pallas_call | solution.py:270
  27.4 1.3 %copy.4 = bf16[1,16,128]{2,1,0:T(8,128)(2,1)} copy(bf16[1,16,128]{2,1,0:T(8,128)(2,1)} %shard_map.28) | data formatting | bytes 8192

commit v3 on v2

--- a/solution.py
+++ b/solution.py
@@ -8,7 +8,7 @@
 from jax.sharding import PartitionSpec as P
 
 MESH = pl.DeviceIdType.MESH
-AHEAD, LOOK = 4, 4
+LOOK = 1
 
 
 def each(low, high, body):
@@ -31,7 +31,7 @@
 
 
 def kernel(
-    n, m, chunks, x_hbm, op_hbm, out_ref, x, op, acc, part, total, share,
+    n, m, chunks, x_hbm, op_hbm, out_ref, x, far, op, acc, part, total, share,
     own_sem, op_sem, out_sem, pair_sem, fwd_sem, relay_sem, in_sem,
     red_out, red_in, floor_out, floor_in,
 ):
@@ -66,6 +66,9 @@
 
     many = max(rows, cols)
 
+    def straight(source, at):
+        return (lax.div(source, cols) == lax.div(at, cols)) | (lax.rem(source, cols) == lax.rem(at, cols))
+
     def relayed(odd, source, block, at, step):
         turn = lax.rem(core + odd, 2) == 0
         r, q = lax.div(source, cols), lax.rem(source, cols)
@@ -80,16 +83,16 @@
         passes = at < 0
         for step in range(1, many):
             passes = passes | relayed(odd, source, block, at, step)[0]
-        straight = (lax.div(source, cols) == lax.div(at, cols)) | (lax.rem(source, cols) == lax.rem(at, cols))
-        return straight & (need(block, at) | passes), passes
+        return straight(source, at) & (need(block, at) | passes), passes
 
     def make_plan(step, odd):
         other = lax.rem(chip + step, chips)
         block = 2 * other + core
         wanted, _ = route(odd, chip, me, other)
         _, passes = route(odd, other, block, chip)
-        here = need(block, chip)
-        alone = here & jnp.logical_not(passes)
+        near = straight(other, chip)
+        here = need(block, chip) & near, need(block, chip) & jnp.logical_not(near)
+        alone = here[0] & jnp.logical_not(passes)
         onward = [relayed(odd, other, block, chip, s) for s in range(1, many)]
         return other, block, wanted, passes, here, alone, onward
 
@@ -101,28 +104,38 @@
         return plans[step, c % 2] if plans else make_plan(step, c % 2)
 
     others = [2 * lax.rem(chip + step, chips) + 1 - core for step in range(chips)] if plans else None
-    others_here = [need(block, chip) for block in others] if plans else None
+    def other_here(block):
+        near = straight(lax.div(block, 2), chip)
+        return need(block, chip) & near, need(block, chip) & jnp.logical_not(near)
+
+    others_here = [other_here(block) for block in others] if plans else None
     self_here = need(me, chip)
 
-    def send(c, block, target, sem, first=False):
+    busy = need(2 * row * cols, chip) | need(2 * col, chip)
+
+    def send(c, block, target, sem, source=None, into=None):
         return pltpu.make_async_remote_copy(
-            src_ref=x_hbm.at[0, :, columns(c)] if first else x.at[c, block], dst_ref=x.at[c, block],
+            src_ref=x.at[c, block] if source is None else source,
+            dst_ref=(x if into is None else into).at[c, block],
             send_sem=sem, recv_sem=in_sem.at[c, block], device_id={"tm": target}, device_id_type=MESH,
         )
 
+    def mine(c):
+        return x_hbm.at[0, :, columns(c)]
+
     def sends(c, act):
         def one(step):
             _, block, wanted, *_ = plan(step, c)
 
             @pl.when(wanted)
             def _():
-                act(send(c, me, block, out_sem.at[c, step], True))
+                act(send(c, me, block, out_sem.at[c, step], mine(c)))
 
         each(1, chips, one)
 
         @pl.when(self_here)
         def _():
-            act(send(c, me, pair, pair_sem.at[c], True))
+            act(send(c, me, pair, pair_sem.at[c], mine(c)))
 
     def relays(c, act, wait):
         def one(step):
@@ -135,7 +148,7 @@
                 for s, (wanted, target) in enumerate(onward):
                     @pl.when(wanted)
                     def _(s=s, target=target):
-                        act(send(c, block, target, relay_sem.at[c, source, s]))
+                        act(send(c, block, target, relay_sem.at[c, source, s], None, far))
 
         each(1, chips, one)
 
@@ -147,20 +160,33 @@
                 def _():
                     send(c, block, pair, fwd_sem.at[c, source]).wait_recv()
 
+            @pl.when(here[0])
+            def _():
+                act(send(c, block, pair, fwd_sem.at[c, source]))
+
+        each(1, chips, one)
+
+    def far_forwards(c, act, wait):
+        def one(step):
+            source, block, _, _, here, _, _ = plan(step, c)
+
+            @pl.when(here[1])
+            def _():
+                copy = send(c, block, pair, fwd_sem.at[c, source], far.at[c, block], far)
+                if wait:
+                    copy.wait_recv()
+                act(copy)
+
+        each(1, chips, one)
+
+    def take(c, part_of):
+        def one(step):
+            block = others[step] if plans else 2 * lax.rem(chip + step, chips) + 1 - core
+            here = (others_here[step] if plans else other_here(block))[part_of]
+
             @pl.when(here)
             def _():
-                act(send(c, block, pair, fwd_sem.at[c, source]))
-
-        each(1, chips, one)
-
-    def take(c):
-        def one(step):
-            block = others[step] if plans else 2 * lax.rem(chip + step, chips) + 1 - core
-            here = others_here[step] if plans else need(block, chip)
-
-            @pl.when(here)
-            def _():
-                send(c, block, pair, pair_sem.at[c]).wait_recv()
+                send(c, block, pair, pair_sem.at[c], None, far if part_of else None).wait_recv()
 
         each(0, chips, one)
 
@@ -170,36 +196,36 @@
     def wait_send(copy):
         copy.wait_send()
 
-    for c in range(min(AHEAD, chunks)):
+
+    tile = min(n, max(1, 128 // k))
+
+    def image_of(block_rows, c):
+        return lax.dot_general(
+            block_rows.reshape(-1, width), op[c], (((1,), (1,)), ((), ())), preferred_element_type=jnp.float32
+        ).reshape(-1, k, sensors)
+
+    for c in range(chunks):
         sends(c, start)
-
-    tile = min(n, max(1, 128 // k))
-
-    def pass_on(c):
-        if c < chunks:
-            relays(c, start, True)
-        if c + AHEAD < chunks:
-            sends(c + AHEAD, start)
-
     for c in range(min(LOOK, chunks)):
-        pass_on(c)
+        relays(c, start, True)
     forwards(0, start, True)
     for c in range(chunks):
-        pass_on(c + LOOK)
+        if c + LOOK < chunks:
+            relays(c + LOOK, start, True)
         if c + 1 < chunks:
             forwards(c + 1, start, True)
-        take(c)
+        take(c, 0)
         own[c].wait()
         weights[c].wait()
-        for r in range(n // tile):
-            block_rows = x[c, r * tile:(r + 1) * tile].reshape(tile * k, width)
-            image = lax.dot_general(
-                block_rows, op[c], (((1,), (1,)), ((), ())), preferred_element_type=jnp.float32
-            ).reshape(tile, k, sensors)
-            if c == 0:
-                acc[r * tile:(r + 1) * tile] = image
-            else:
-                acc[r * tile:(r + 1) * tile] += image
+
+        @pl.when(busy)
+        def _(c=c):
+            for r in range(n // tile):
+                image = image_of(x[c, r * tile:(r + 1) * tile], c)
+                if c == 0:
+                    acc[r * tile:(r + 1) * tile] = image
+                else:
+                    acc[r * tile:(r + 1) * tile] += image
 
     def lag_part(step):
         return pltpu.make_async_remote_copy(
@@ -208,15 +234,42 @@
             device_id={"tm": lax.rem(me + step, n)}, device_id_type=MESH,
         )
 
-    for step in range(n - 1, 0, -1):
-        @pl.when(me + step < n)
-        def _(step=step):
-            lag_part(step).start()
+    def lag_parts(near, act):
+        for step in range(n - 1, 0, -1):
+            @pl.when((me + step < n) & (straight(step // 2, chip) == near))
+            def _(step=step):
+                act(lag_part(step))
+
+    lag_parts(True, start)
+
+    far_forwards(0, start, True)
+    for c in range(chunks):
+        if c + 1 < chunks:
+            far_forwards(c + 1, start, True)
+        take(c, 1)
+
+        def far_images(step, c=c):
+            r = lax.rem(row + 1 + lax.div(step, max(1, cols - 1)), rows)
+            q = lax.rem(col + 1 + lax.rem(step, max(1, cols - 1)), cols)
+            source = r * cols + q
+
+            @pl.when(need(2 * source, chip))
+            def _():
+                image = image_of(far[c, pl.ds(2 * source, 2)], c)
+                if c == 0:
+                    acc[pl.ds(2 * source, 2)] = image
+                else:
+                    acc[pl.ds(2 * source, 2)] += image
+
+        each(0, (rows - 1) * (cols - 1), far_images)
+
+    lag_parts(False, start)
 
     for c in range(chunks):
         sends(c, wait_send)
         relays(c, wait_send, False)
         forwards(c, wait_send, False)
+        far_forwards(c, wait_send, False)
 
     def add_lag(lag, value):
         pltpu.make_async_remote_copy(
@@ -251,10 +304,8 @@
         result = result + share[source]
     out_ref[0] = result.astype(out_ref.dtype)
 
-    for step in range(n - 1, 0, -1):
-        @pl.when(me + step < n)
-        def _(step=step):
-            lag_part(step).wait_send()
+    lag_parts(True, wait_send)
+    lag_parts(False, wait_send)
     for step in range(1, m):
         to_floor(step).wait_send()
 
@@ -273,6 +324,7 @@
             in_specs=[pl.BlockSpec(memory_space=pl.ANY)] * 2,
             out_specs=pl.BlockSpec(memory_space=pltpu.VMEM),
             scratch_shapes=[
+                pltpu.VMEM((chunks, n, k, width), jnp.bfloat16),
                 pltpu.VMEM((chunks, n, k, width), jnp.bfloat16),
                 pltpu.VMEM((chunks, sensors, width), jnp.bfloat16),
                 pltpu.VMEM((n, k, sensors), jnp.float32),

time: 28.9 us -> 28.2 us (0.976)
  the two profiles are of different devices: /device:TPU:2 before, /device:TPU:6 now
where the time goes in v3:
time: 28.2 us; the launch traced here: 28 us
  Pallas kernels  26.7 us (95%)
  local copies, waits for them, and re-layouts  1.28 us (5%)
    pallas_call x1, Pallas kernels, local(): pl.pallas_call(functools.partial(kernel, n, m, chunks), out_shape=jax.Sha...  26.7 us
    unnamed x1, local copies, waits for them, and re-layouts  1.28 us

profile of v3, /device:TPU:6, one launch (start us, length us, event | category | flops | bytes accessed | tf_op | source)
XLA Modules:
  0.0 28.0 jit_solution(11282581036022915950)
XLA Ops:
  0.0 26.7 %shard_map.28 = bf16[1,16,128]{2,1,0:T(8,128)(2,1)} custom-call(bf16[1,16,8192]{2,1,0:T(8,128)(2,1)} %x_hbm.1, bf16[1,512,8192]{2,1,0:T(8,128)(2,1)} %op_hbm.1), custom_call_target="tpu_custom_call" | custom-call | tf_op jit(solution)/shard_map/pallas_call | solution.py:321
  26.7 1.3 %copy.4 = bf16[1,16,128]{2,1,0:T(8,128)(2,1)} copy(bf16[1,16,128]{2,1,0:T(8,128)(2,1)} %shard_map.28) | data formatting | bytes 8192

commit v4 on v3

--- a/solution.py
+++ b/solution.py
@@ -33,7 +33,7 @@
 def kernel(
     n, m, chunks, x_hbm, op_hbm, out_ref, x, far, op, acc, part, total, share,
     own_sem, op_sem, out_sem, pair_sem, fwd_sem, relay_sem, in_sem,
-    red_out, red_in, floor_out, floor_in,
+    red_out, red_in, floor_out, floor_in, up_sem, down_sem,
 ):
     me, floor = lax.axis_index("tm"), lax.axis_index("floor")
     chips = n // 2
@@ -57,9 +57,26 @@
     barrier = pltpu.get_barrier_semaphore()
     for step in range(1, n):
         pl.semaphore_signal(barrier, inc=1, device_id={"tm": lax.rem(me + step, n)}, device_id_type=MESH)
-    for step in range(1, m):
-        pl.semaphore_signal(barrier, inc=1, device_id={"floor": lax.rem(floor + step, m)}, device_id_type=MESH)
-    pl.semaphore_wait(barrier, n + m - 2)
+    below, above = floor > 0, floor < m - 1
+
+    @pl.when(below)
+    def _():
+        pl.semaphore_signal(barrier, inc=1, device_id={"floor": floor - 1}, device_id_type=MESH)
+
+    @pl.when(above)
+    def _():
+        pl.semaphore_signal(barrier, inc=1, device_id={"floor": floor + 1}, device_id_type=MESH)
+
+    pl.semaphore_wait(barrier, n - 1 + jnp.where(below, 1, 0) + jnp.where(above, 1, 0))
+
+    def words(turn):
+        for sem, place, target in ((up_sem, floor, floor + 1), (down_sem, m - 1 - floor, floor - 1)):
+            @pl.when(place == turn)
+            def _(sem=sem, target=target):
+                if turn > 0:
+                    pl.semaphore_wait(sem, 1)
+                if turn < m - 1:
+                    pl.semaphore_signal(sem, inc=1, device_id={"floor": target}, device_id_type=MESH)
 
     def need(block, at_chip):
         return 2 * at_chip + block < n
@@ -215,6 +232,8 @@
         if c + 1 < chunks:
             forwards(c + 1, start, True)
         take(c, 0)
+        if c < m:
+            words(c)
         own[c].wait()
         weights[c].wait()
 
@@ -241,6 +260,8 @@
                 act(lag_part(step))
 
     lag_parts(True, start)
+    for turn in range(chunks, m):
+        words(turn)
 
     far_forwards(0, start, True)
     for c in range(chunks):
@@ -342,6 +363,8 @@
                 pltpu.SemaphoreType.DMA((n,)),
                 pltpu.SemaphoreType.DMA((m,)),
                 pltpu.SemaphoreType.DMA((m,)),
+                pltpu.SemaphoreType.REGULAR,
+                pltpu.SemaphoreType.REGULAR,
             ],
             compiler_params=pltpu.CompilerParams(collective_id=0, has_side_effects=True),
         )(samples, operator)

time: 28.2 us -> 28.2 us (level)
  no operation moved by 1% of the time
where the time goes in v4:
time: 28.2 us; the launch traced here: 28 us
  Pallas kernels  26.8 us (95%)
  local copies, waits for them, and re-layouts  1.28 us (5%)
    pallas_call x1, Pallas kernels, local(): pl.pallas_call(functools.partial(kernel, n, m, chunks), out_shape=jax.Sha...  26.8 us
    unnamed x1, local copies, waits for them, and re-layouts  1.28 us

profile of v4, /device:TPU:6, one launch (start us, length us, event | category | flops | bytes accessed | tf_op | source)
XLA Modules:
  0.0 28.0 jit_solution(9056569344895715062)
XLA Ops:
  0.0 26.8 %shard_map.28 = bf16[1,16,128]{2,1,0:T(8,128)(2,1)} custom-call(bf16[1,16,8192]{2,1,0:T(8,128)(2,1)} %x_hbm.1, bf16[1,512,8192]{2,1,0:T(8,128)(2,1)} %op_hbm.1), custom_call_target="tpu_custom_call" | custom-call | tf_op jit(solution)/shard_map/pallas_call | solution.py:342
  26.8 1.3 %copy.4 = bf16[1,16,128]{2,1,0:T(8,128)(2,1)} copy(bf16[1,16,128]{2,1,0:T(8,128)(2,1)} %shard_map.28) | data formatting | bytes 8192

commit v5 on v4

--- a/solution.py
+++ b/solution.py
@@ -286,12 +286,6 @@
 
     lag_parts(False, start)
 
-    for c in range(chunks):
-        sends(c, wait_send)
-        relays(c, wait_send, False)
-        forwards(c, wait_send, False)
-        far_forwards(c, wait_send, False)
-
     def add_lag(lag, value):
         pltpu.make_async_remote_copy(
             src_ref=acc.at[0], dst_ref=part.at[lag],
@@ -314,6 +308,14 @@
 
     for step in range(m - 1, 0, -1):
         to_floor(step).start()
+    for c in range(chunks):
+        sends(c, wait_send)
+        relays(c, wait_send, False)
+        forwards(c, wait_send, False)
+        far_forwards(c, wait_send, False)
+
+    lag_parts(True, wait_send)
+    lag_parts(False, wait_send)
     result = total[floor]
     for step in range(1, m):
         source = lax.rem(floor + step, m)
@@ -325,8 +327,6 @@
         result = result + share[source]
     out_ref[0] = result.astype(out_ref.dtype)
 
-    lag_parts(True, wait_send)
-    lag_parts(False, wait_send)
     for step in range(1, m):
         to_floor(step).wait_send()
 

time: 28.2 us -> 28.2 us (level)
  no operation moved by 1% of the time
where the time goes in v5:
time: 28.2 us; the launch traced here: 28 us
  Pallas kernels  26.8 us (95%)
  local copies, waits for them, and re-layouts  1.28 us (5%)
    pallas_call x1, Pallas kernels, local(): pl.pallas_call(functools.partial(kernel, n, m, chunks), out_shape=jax.Sha...  26.8 us
    unnamed x1, local copies, waits for them, and re-layouts  1.28 us

profile of v5, /device:TPU:6, one launch (start us, length us, event | category | flops | bytes accessed | tf_op | source)
XLA Modules:
  0.0 28.0 jit_solution(1762832234760899540)
XLA Ops:
  0.0 26.8 %shard_map.28 = bf16[1,16,128]{2,1,0:T(8,128)(2,1)} custom-call(bf16[1,16,8192]{2,1,0:T(8,128)(2,1)} %x_hbm.1, bf16[1,512,8192]{2,1,0:T(8,128)(2,1)} %op_hbm.1), custom_call_target="tpu_custom_call" | custom-call | tf_op jit(solution)/shard_map/pallas_call | solution.py:342
  26.8 1.3 %copy.4 = bf16[1,16,128]{2,1,0:T(8,128)(2,1)} copy(bf16[1,16,128]{2,1,0:T(8,128)(2,1)} %shard_map.28) | data formatting | bytes 8192
